TPU v7x, 32 devices: a whole 2x2x4 slice. The times are simulated.
32 devices in a mesh: lat: 4 (over y, x), lon: 4 (over z), var: 2 (over core).
Axes of the slice: x: 2, y: 2, z: 4, core: 2. Of those that a mesh axis runs over, the one named last changes fastest.
Arguments:
- control: float32 [6, 4, 128, 512], P('var', None, 'lat', 'lon'), may hold values from -6 to 6
- gradient: float32 [6, 4, 128, 512], P('var', None, 'lat', 'lon'), may hold values from -6 to 6
- std_dev: float32 [6, 128, 512], P('var', 'lat', 'lon'), may hold values from 0.3 to 3
- sea_mask: int32 [128, 512], P('lat', 'lon'), may hold values 0 or 1
- x_taps: float32 [6, 21], P('var'), may hold values from 0.02 to 0.3
- y_taps: float32 [6, 21], P('var'), may hold values from 0.02 to 0.3
- z_taps: float32 [6, 4], P('var'), may hold values from 0.05 to 0.5
- column_weight: float32 [3, 4], replicated, may hold values from 0.1 to 0.5
- balance: float32 [3, 3, 4], replicated, may hold values from -1.5 to 1.5
Outputs:
- increment: float32 [6, 4, 128, 512], P('var', None, 'lat', 'lon')
- control_gradient: float32 [6, 4, 128, 512], P('var', None, 'lat', 'lon')
All inputs are finite; a program needn't handle non-finite values. No bound on the sum of `sea_mask` on one device may be relied on, other than what follows from the above.
Results may differ from a plain program's by a relative error of at most 0.00007.
Values sent between devices are 32-bit elements; how exact they have to be, the bound alone decides.
A program may use at most 64 MiB of HBM per device.

v0:
```python
import functools
import jax
import jax.numpy as jnp
from jax import lax
from jax.experimental import pallas as pl
from jax.experimental.pallas import tpu as pltpu
from jax.sharding import PartitionSpec as P

F32 = jnp.float32
BF16 = jnp.bfloat16
MESH = pl.DeviceIdType.MESH


def halves(value):
    high = value.astype(BF16)
    low = (value - high.astype(F32)).astype(BF16)
    return high, low


def dot(left, right):
    return jnp.dot(left, right, preferred_element_type=F32)


def tap_select(distance, taps, var, radius):
    total = jnp.zeros(distance.shape, F32)
    for tap in range(radius + 1):
        total = jnp.where(distance == tap, taps[var, tap], total)
    return total


def kernel(
    sizes,
    control_hbm, gradient_hbm, std_hbm, mask_hbm, xt, yt, zt, cw, bal,
    inc_ref, cg_ref,
    con, gra, std, mask, bands_x, bands_y, rows_out, rows_in, lanes_out, lanes_in,
    pad, col_out, col_in,
    relay, fold, load_sem, rows_ss, rows_rs, relay_ss, relay_rs, fold_ss, fold_rs, lanes_ss, lanes_rs, col_ss, col_rs,
):
    lats, lons, radius = sizes
    nv, nz, ny, nx = con.shape
    half = nz // 2
    lat, lon, var = lax.axis_index("lat"), lax.axis_index("lon"), lax.axis_index("var")
    top, bottom, upper = lat == lats - 1, lat == 0, var == 1
    east, west = lax.rem(lon + 1, lons), lax.rem(lon + lons - 1, lons)
    mirror = lons - 1 - lon
    other = 1 - var
    relays = lats >= 4 and lats % 2 == 0
    parity = lax.rem(lat, 2)
    step = 2 * parity - 1
    ahead, behind = lat + 2 * step, lat - 2 * step
    turning = (ahead >= 0) & (ahead < lats) & relays
    relaying = (behind >= 0) & (behind < lats) & relays
    spread = jnp.abs(lons - 1 - 2 * lon)
    far = (spread > 1) & relays
    folding = far & (lat == lats - 3)
    chunk = nz * radius // 2

    def rdma(src, dst, ss, rs, where):
        return pltpu.make_async_remote_copy(
            src_ref=src, dst_ref=dst, send_sem=ss, recv_sem=rs, device_id=where, device_id_type=MESH
        )

    loads = [
        pltpu.make_async_copy(src, dst, load_sem.at[i])
        for i, (src, dst) in enumerate(
            ((control_hbm, con), (gradient_hbm, gra), (std_hbm, std), (mask_hbm, mask))
        )
    ]
    for load in loads:
        load.start()

    barrier = pltpu.get_barrier_semaphore()
    pl.semaphore_signal(barrier, inc=1, device_id={"lon": east}, device_id_type=MESH)
    pl.semaphore_signal(barrier, inc=1, device_id={"lon": west}, device_id_type=MESH)
    pl.semaphore_signal(barrier, inc=1, device_id={"var": other}, device_id_type=MESH)

    def greet(condition, where):
        @pl.when(condition)
        def _():
            pl.semaphore_signal(barrier, inc=1, device_id=where, device_id_type=MESH)

    greet(top, {"lon": mirror})
    greet(turning, {"lat": ahead})
    greet(relaying, {"lat": behind})
    greet(top & far, {"lat": lat - 2, "lon": mirror})
    greet(folding, {"lat": lat + 2, "lon": mirror})

    @pl.when(jnp.logical_not(top))
    def _():
        pl.semaphore_signal(barrier, inc=1, device_id={"lat": lat + 1}, device_id_type=MESH)

    @pl.when(jnp.logical_not(bottom))
    def _():
        pl.semaphore_signal(barrier, inc=1, device_id={"lat": lat - 1}, device_id_type=MESH)

    lane = lax.broadcasted_iota(jnp.int32, (half * ny, nx), 1)
    backwards = nx - 1 - lax.broadcasted_iota(jnp.int32, (ny, nx), 1)

    def part(h):
        return pl.ds(h * chunk, chunk)

    def send_rows(field, v):
        for h in (1, 0):
            def go(condition, way, dst, rs, where, h=h):
                @pl.when(condition)
                def _():
                    rdma(rows_out.at[field, way, v, part(h)], dst, rows_ss.at[field, way, v, h], rs, where).start()

            up, down = rows_in.at[field, 0, v, part(h)], rows_in.at[field, 1, v, part(h)]
            up_rs, down_rs = rows_rs.at[field, 0, v, h], rows_rs.at[field, 1, v, h]
            below_top = jnp.logical_not(top)
            off_bottom = jnp.logical_not(bottom)
            if h == 1:
                go(top & far, 0, fold.at[field, v], fold_rs.at[field, v], {"lat": lat - 2})
            go(top & jnp.logical_not(far) if h == 1 else top, 0, down, down_rs, {"lon": mirror})
            if h == 1 and relays:
                odd = parity == 1
                go(below_top & odd, 0, relay.at[field, v], relay_rs.at[field, v], {"lat": lat + 2})
                go(off_bottom & jnp.logical_not(odd), 1, relay.at[field, v], relay_rs.at[field, v], {"lat": lat - 2})
                below_top = below_top & jnp.logical_not(odd)
                off_bottom = off_bottom & odd
            go(below_top, 0, up, up_rs, {"lat": lat + 1})
            go(off_bottom, 1, down, down_rs, {"lat": lat - 1})

    def any_rows(field, way, v, h):
        return rdma(rows_out.at[field, way, v, part(h)], rows_in.at[field, way, v, part(h)],
                    rows_ss.at[field, way, v, h], rows_rs.at[field, way, v, h], {"lon": east})

    def relay_copy(field, v):
        way = 1 - parity
        return rdma(relay.at[field, v], rows_in.at[field, way, v, part(1)], relay_ss.at[field, v],
                    rows_rs.at[field, way, v, 1], {"lat": lat - step})

    def relay_arrival(field, v):
        return rdma(relay.at[field, v], relay.at[field, v], relay_ss.at[field, v], relay_rs.at[field, v],
                    {"lon": east})

    def fold_copy(field, v):
        return rdma(fold.at[field, v], rows_in.at[field, 1, v, part(1)], fold_ss.at[field, v],
                    rows_rs.at[field, 1, v, 1], {"lat": lat + 2, "lon": mirror})

    def fold_arrival(field, v):
        return rdma(fold.at[field, v], fold.at[field, v], fold_ss.at[field, v], fold_rs.at[field, v],
                    {"lon": east})

    def pass_rows(field):
        if not relays:
            return
        for v in range(nv):
            @pl.when(relaying)
            def _():
                relay_arrival(field, v).wait_recv()
                relay_copy(field, v).start()

        @pl.when(folding)
        def _():
            for v in range(nv):
                fold_arrival(field, v).wait_recv()
                fold_copy(field, v).start()

    def pack_rows(field, v, planes):
        for z in range(nz):
            rows_out[field, 1, v, z * radius:(z + 1) * radius] = planes[z][:radius]

        @pl.when(top)
        def _():
            for z in range(nz):
                turned = jnp.take_along_axis(planes[z], backwards, axis=1)
                rows_out[field, 0, v, z * radius:(z + 1) * radius] = turned[ny - radius - 1:ny - 1]

        @pl.when(jnp.logical_not(top))
        def _():
            for z in range(nz):
                rows_out[field, 0, v, z * radius:(z + 1) * radius] = planes[z][ny - radius:]

    def pack_lanes(field, flats):
        last = jnp.zeros((half * ny, nx), F32)
        first = jnp.zeros((half * ny, nx), F32)
        for h in range(2):
            for v in range(nv):
                start = (h * nv + v) * radius
                inside = (lane >= start) & (lane < start + radius)
                block = flats[v][h * half * ny:(h + 1) * half * ny]
                last = jnp.where(inside, pltpu.roll(block, (start - (nx - radius)) % nx, 1), last)
                first = jnp.where(inside, pltpu.roll(block, start, 1) if start else block, first)
        lanes_out[field, 0] = last
        lanes_out[field, 1] = first

    def lanes_copy(field, side):
        return rdma(lanes_out.at[field, side], lanes_in.at[field, side], lanes_ss.at[field, side],
                    lanes_rs.at[field, side], {"lon": east if side == 0 else west})

    def filter_x(field, v, flat):
        last, first = lanes_in[field, 0], lanes_in[field, 1]
        wraps = []
        for h in range(2):
            start = (h * nv + v) * radius
            from_west = pltpu.roll(last, (nx - radius - start) % nx, 1)
            from_east = pltpu.roll(first, (-start) % nx, 1) if start else first
            wraps.append(jnp.where(lane >= nx - radius, from_west, jnp.where(lane < radius, from_east, 0.0)))
        high, low = halves(jnp.concatenate([flat, jnp.concatenate(wraps, axis=0)], axis=1))
        both = dot(high, bands_x[v])
        return both[:, :nx] + both[:, nx:] + dot(low, bands_x[v, :, :nx])

    span = ny + 2 * radius

    def filter_y(field, v, planes):
        for z in range(nz):
            cols = slice(z * nx, (z + 1) * nx)
            part = slice(z * radius, (z + 1) * radius)
            pad[v, :ny, cols] = planes[z]
            pad[v, ny:ny + radius, cols] = rows_in[field, 0, v, part]
            pad[v, ny + radius:span, cols] = rows_in[field, 1, v, part]
        high, low = halves(pad[v])
        both = dot(bands_y[v, :, :span], high)
        return both[:ny] + both[ny:] + dot(bands_y[v, :ny, :span], low)

    def filter_z(v, levels):
        out = []
        for z in range(nz):
            total = zt[v, z] * levels[0]
            for w in range(1, nz):
                total = total + zt[v, abs(z - w)] * levels[w]
            out.append(total)
        return out

    @pl.when(bottom)
    def _():
        rows_in[:, 0] = jnp.zeros(rows_in.shape[:1] + rows_in.shape[2:], F32)

    loads[0].wait()
    for v in range(nv):
        pack_rows(0, v, [con[v, z] for z in range(nz)])
    loads[1].wait()

    @pl.when(upper)
    def _():
        for b in range(nv):
            total = jnp.zeros((ny, nx), F32)
            for a in range(nv):
                for z in range(nz):
                    total = total + bal[a, b, z] * gra[a, z]
            col_out[0, b] = total

    def col_copy(which):
        return rdma(col_out.at[which], col_in.at[which], col_ss.at[which], col_rs.at[which], {"var": other})

    count = lambda condition: jnp.where(condition, 1, 0)
    greeted = 4 + count(jnp.logical_not(bottom))
    greeted = greeted + count(turning) + count(relaying) + count((top & far) | folding)
    pl.semaphore_wait(barrier, greeted)

    @pl.when(upper)
    def _():
        col_copy(0).start()

    for v in range(nv):
        send_rows(0, v)

    loads[2].wait()
    loads[3].wait()
    sea = mask[...].astype(F32)
    for v in range(nv):
        std[v] = std[v] * sea

    @pl.when(upper)
    def _():
        for v in range(nv):
            for z in range(nz):
                gra[v, z] = gra[v, z] * std[v]

    @pl.when(jnp.logical_not(upper))
    def _():
        col_copy(0).wait_recv()
        for v in range(nv):
            for z in range(nz):
                gra[v, z] = (gra[v, z] + cw[v, z] * col_in[0, v]) * std[v]

    flats = [gra[v].reshape(nz * ny, nx) for v in range(nv)]
    pack_lanes(1, flats)
    for side in range(2):
        lanes_copy(1, side).start()

    circle = lax.broadcasted_iota(jnp.int32, (8, nx), 1)
    circle = jnp.minimum(circle, nx - circle)
    apart = jnp.abs(
        lax.broadcasted_iota(jnp.int32, (nx, nx), 0) - lax.broadcasted_iota(jnp.int32, (nx, nx), 1)
    )
    row = lax.broadcasted_iota(jnp.int32, (ny, nx), 0)
    slot = lax.broadcasted_iota(jnp.int32, (ny, nx), 1)
    below = jnp.where(bottom, 2 * span, row + radius - (slot - ny))
    beyond = slot - (ny + radius)
    above = jnp.where(top, ny - 1 + radius - beyond - row, ny + beyond - row)
    distance = jnp.where(slot < ny, jnp.abs(row - slot), jnp.where(slot < ny + radius, below, above))
    distance = jnp.where(slot < span, distance, 2 * span)
    for v in range(nv):
        ring = tap_select(circle, xt, v, radius)
        full = pltpu.roll(jnp.broadcast_to(ring[:1], (nx, nx)), 0, 1, stride=1, stride_axis=0)
        near = jnp.where(apart <= radius, full, 0.0)
        wrap = jnp.where(apart <= radius, 0.0, full)
        bands_x[v, :nx, :nx], bands_x[v, :nx, nx:] = halves(near)
        bands_x[v, nx:, :nx], bands_x[v, nx:, nx:] = halves(wrap)
        band = tap_select(distance, yt, v, radius)
        number = var * nv + v
        sign = jnp.where(top & ((number == 3) | (number == 4)), -1.0, 1.0).astype(F32)
        band = jnp.where(slot >= ny + radius, band * sign, band)
        bands_y[v, :ny], bands_y[v, ny:] = halves(band)

    pass_rows(0)
    for side in range(2):
        lanes_copy(1, side).wait_recv()
    for v in range(nv):
        flat = filter_x(1, v, gra[v].reshape(nz * ny, nx))
        gra[v] = flat.reshape(nz, ny, nx)
        pack_rows(1, v, [flat[z * ny:(z + 1) * ny] for z in range(nz)])
        send_rows(1, v)

    def wait_rows(field, v):
        for h in range(2):
            any_rows(field, 1, v, h).wait_recv()

        @pl.when(jnp.logical_not(bottom))
        def _():
            for h in range(2):
                any_rows(field, 0, v, h).wait_recv()

    flats = []
    for v in range(nv):
        wait_rows(0, v)
        out = filter_y(0, v, [con[v, z] for z in range(nz)])
        for z in range(nz):
            con[v, z] = out[:, z * nx:(z + 1) * nx]
    pack_lanes(0, [con[v].reshape(nz * ny, nx) for v in range(nv)])
    for side in range(2):
        lanes_copy(0, side).start()
    pass_rows(1)
    for side in range(2):
        lanes_copy(0, side).wait_recv()
    for v in range(nv):
        flat = filter_x(0, v, con[v].reshape(nz * ny, nx))
        levels = filter_z(v, [flat[z * ny:(z + 1) * ny] for z in range(nz)])
        total = jnp.zeros((ny, nx), F32)
        for z in range(nz):
            shaped = levels[z] * std[v]
            con[v, z] = shaped
            inc_ref[v, z] = shaped
            total = total + cw[v, z] * shaped
        col_out[1, v] = total

    @pl.when(jnp.logical_not(upper))
    def _():
        col_copy(1).start()

    for v in range(nv):
        wait_rows(1, v)
        out = filter_y(1, v, [gra[v, z] for z in range(nz)])
        levels = filter_z(v, [out[:, z * nx:(z + 1) * nx] for z in range(nz)])
        for z in range(nz):
            cg_ref[v, z] = levels[z]

    @pl.when(upper)
    def _():
        col_copy(1).wait_recv()
        for a in range(nv):
            for z in range(nz):
                total = con[a, z]
                for b in range(nv):
                    total = total + bal[a, b, z] * col_in[1, b]
                inc_ref[a, z] = total
        col_copy(0).wait_send()

    @pl.when(jnp.logical_not(upper))
    def _():
        col_copy(1).wait_send()

    for field in range(2):
        for side in range(2):
            lanes_copy(field, side).wait_send()
        for v in range(nv):
            for h in range(2):
                any_rows(field, 0, v, h).wait_send()

            @pl.when(jnp.logical_not(bottom))
            def _():
                for h in range(2):
                    any_rows(field, 1, v, h).wait_send()

            if relays:
                @pl.when(relaying)
                def _():
                    relay_copy(field, v).wait_send()

                @pl.when(folding)
                def _():
                    fold_copy(field, v).wait_send()


def per_device(lats, lons, control, gradient, std_dev, sea_mask, x_taps, y_taps, z_taps, column_weight, balance):
    nv, nz, ny, nx = control.shape
    radius = x_taps.shape[1] - 1
    span = ny + 2 * radius
    anywhere = pl.BlockSpec(memory_space=pl.ANY)
    scalars = pl.BlockSpec(memory_space=pltpu.SMEM)
    vmem = pl.BlockSpec(memory_space=pltpu.VMEM)
    dma = pltpu.SemaphoreType.DMA
    return pl.pallas_call(
        functools.partial(kernel, (lats, lons, radius)),
        out_shape=(pltpu.VMEM(control.shape, F32),) * 2,
        in_specs=[anywhere] * 4 + [scalars] * 5,
        out_specs=(vmem, vmem),
        scratch_shapes=[
            pltpu.VMEM(control.shape, F32),
            pltpu.VMEM(control.shape, F32),
            pltpu.VMEM(std_dev.shape, F32),
            pltpu.VMEM(sea_mask.shape, jnp.int32),
            pltpu.VMEM((nv, 2 * nx, 2 * nx), BF16),
            pltpu.VMEM((nv, 2 * ny, nx), BF16),
            pltpu.VMEM((2, 2, nv, nz * radius, nx), F32),
            pltpu.VMEM((2, 2, nv, nz * radius, nx), F32),
            pltpu.VMEM((2, 2, nz // 2 * ny, nx), F32),
            pltpu.VMEM((2, 2, nz // 2 * ny, nx), F32),
            pltpu.VMEM((nv, span, nz * nx), F32),
            pltpu.VMEM((2, nv, ny, nx), F32),
            pltpu.VMEM((2, nv, ny, nx), F32),
            pltpu.VMEM((2, nv, nz * radius // 2, nx), F32),
            pltpu.VMEM((2, nv, nz * radius // 2, nx), F32),
            dma((4,)),
            dma((2, 2, nv, 2)),
            dma((2, 2, nv, 2)),
            dma((2, nv)),
            dma((2, nv)),
            dma((2, nv)),
            dma((2, nv)),
            dma((2, 2)),
            dma((2, 2)),
            dma((2,)),
            dma((2,)),
        ],
        compiler_params=pltpu.CompilerParams(collective_id=0, has_side_effects=True),
    )(control, gradient, std_dev, sea_mask, x_taps, y_taps, z_taps, column_weight, balance)


def solution(mesh):
    in_specs = (
        P("var", None, "lat", "lon"),
        P("var", None, "lat", "lon"),
        P("var", "lat", "lon"),
        P("lat", "lon"),
        P("var", None),
        P("var", None),
        P("var", None),
        P(),
        P(),
    )
    out_specs = (P("var", None, "lat", "lon"), P("var", None, "lat", "lon"))
    body = functools.partial(per_device, mesh.shape["lat"], mesh.shape["lon"])
    return jax.shard_map(body, mesh=mesh, in_specs=in_specs, out_specs=out_specs, check_vma=False)
```

profile of v0, /device:TPU:7, one launch (start us, length us, event | category | flops | bytes accessed | tf_op | source)
XLA Modules:
  0.0 20.8 jit_solution(10931841277670386748)
XLA Ops:
  0.6 18.8 %shard_map.104 = (f32[3,4,32,128]{3,2,1,0:T(8,128)S(1)}, f32[3,4,32,128]{3,2,1,0:T(8,128)S(1)}) custom-call(f32[3,4,32,128]{3,2,1,0:T(8,128)} %control_hbm.1, f32[3,4,32,128]{3,2,1,0:T(8,128)} %gradient_hbm.1, f32[3,32,128]{2,1,0:T(8,128)} %std_hbm.1, s32[32,128]{1,0:T(8,128)} %mask_hbm.1, f32[3,21]{1,0:T(4,128)} %xt.1, f32[3,21]{1,0:T(4,128)} %yt.1, ...), custom_call_target="tpu_custom_call" | custom-call | tf_op jit(solution)/shard_map/pallas_call | solution.py:406
  19.5 0.7 %copy.13 = f32[3,4,32,128]{3,2,1,0:T(8,128)} copy(f32[3,4,32,128]{3,2,1,0:T(8,128)S(1)} %get-tuple-element.2) | data formatting | bytes 393216
  20.2 0.7 %copy.14 = f32[3,4,32,128]{3,2,1,0:T(8,128)} copy(f32[3,4,32,128]{3,2,1,0:T(8,128)S(1)} %get-tuple-element.3) | data formatting | bytes 393216
where the time goes:
time: 21.1 us; the launch traced here: 20.8 us
  Pallas kernels  18.8 us (89%)
  local copies, waits for them, and re-layouts  1.36 us (6%)
  between operations  0.64 us (3%)
    pallas_call x1, Pallas kernels, per_device(): pl.pallas_call(functools.partial(kernel, (lats, lons, radius)), out_shape...  18.8 us
    unnamed x2, local copies, waits for them, and re-layouts  1.36 us

commit v1 on v0

--- a/solution.py
+++ b/solution.py
@@ -30,11 +30,11 @@
 
 def kernel(
     sizes,
-    control_hbm, gradient_hbm, std_hbm, mask_hbm, xt, yt, zt, cw, bal,
+    control_hbm, gradient_hbm, std_hbm, mask_hbm, xt_hbm, yt_hbm, zt_hbm, cw_hbm, bal_hbm,
     inc_ref, cg_ref,
-    con, gra, std, mask, bands_x, bands_y, rows_out, rows_in, lanes_out, lanes_in,
+    xt, yt, zt, cw, bal, con, gra, std, mask, bands_x, bands_y, rows_out, rows_in, lanes_out, lanes_in,
     pad, col_out, col_in,
-    relay, fold, load_sem, rows_ss, rows_rs, relay_ss, relay_rs, fold_ss, fold_rs, lanes_ss, lanes_rs, col_ss, col_rs,
+    relay, fold, load_sem, rows_ss, rows_rs, relay_ss, relay_rs, fold_ss, fold_rs, lanes_ss, lanes_rs, col_ss, col_rs, token,
 ):
     lats, lons, radius = sizes
     nv, nz, ny, nx = con.shape
@@ -50,8 +50,7 @@
     ahead, behind = lat + 2 * step, lat - 2 * step
     turning = (ahead >= 0) & (ahead < lats) & relays
     relaying = (behind >= 0) & (behind < lats) & relays
-    spread = jnp.abs(lons - 1 - 2 * lon)
-    far = (spread > 1) & relays
+    far = (mirror != lon) & relays
     folding = far & (lat == lats - 3)
     chunk = nz * radius // 2
 
@@ -63,15 +62,17 @@
     loads = [
         pltpu.make_async_copy(src, dst, load_sem.at[i])
         for i, (src, dst) in enumerate(
-            ((control_hbm, con), (gradient_hbm, gra), (std_hbm, std), (mask_hbm, mask))
+            (
+                (control_hbm, con), (gradient_hbm, gra), (std_hbm, std), (mask_hbm, mask),
+                (xt_hbm, xt), (yt_hbm, yt), (zt_hbm, zt), (cw_hbm, cw), (bal_hbm, bal),
+            )
         )
     ]
     for load in loads:
         load.start()
 
     barrier = pltpu.get_barrier_semaphore()
-    pl.semaphore_signal(barrier, inc=1, device_id={"lon": east}, device_id_type=MESH)
-    pl.semaphore_signal(barrier, inc=1, device_id={"lon": west}, device_id_type=MESH)
+    off_top, off_bottom = jnp.logical_not(top), jnp.logical_not(bottom)
     pl.semaphore_signal(barrier, inc=1, device_id={"var": other}, device_id_type=MESH)
 
     def greet(condition, where):
@@ -79,19 +80,28 @@
         def _():
             pl.semaphore_signal(barrier, inc=1, device_id=where, device_id_type=MESH)
 
-    greet(top, {"lon": mirror})
-    greet(turning, {"lat": ahead})
-    greet(relaying, {"lat": behind})
-    greet(top & far, {"lat": lat - 2, "lon": mirror})
-    greet(folding, {"lat": lat + 2, "lon": mirror})
-
-    @pl.when(jnp.logical_not(top))
-    def _():
-        pl.semaphore_signal(barrier, inc=1, device_id={"lat": lat + 1}, device_id_type=MESH)
-
-    @pl.when(jnp.logical_not(bottom))
-    def _():
-        pl.semaphore_signal(barrier, inc=1, device_id={"lat": lat - 1}, device_id_type=MESH)
+    greet(off_top, {"lat": lat + 1, "var": 0})
+    greet(off_bottom, {"lat": lat - 1, "var": 0})
+    greet(turning, {"lat": ahead, "var": 0})
+    greet(relaying, {"lat": behind, "var": 0})
+    pl.semaphore_signal(barrier, inc=1, device_id={"lon": east, "var": 1}, device_id_type=MESH)
+    pl.semaphore_signal(barrier, inc=1, device_id={"lon": west, "var": 1}, device_id_type=MESH)
+    greet(top, {"lon": mirror, "var": 1})
+    greet(top & far, {"lat": lat - 2, "lon": mirror, "var": 1})
+    greet(folding, {"lat": lat + 2, "lon": mirror, "var": 1})
+    count = lambda condition: jnp.where(condition, 1, 0)
+    greeted_lat = 1 + 2 * (count(off_top) + count(off_bottom) + count(turning) + count(relaying))
+    greeted_lon = 5 + 2 * (count(top) + count((top & far) | folding))
+
+    def hear(mine, greeted):
+        @pl.when(mine)
+        def _():
+            pl.semaphore_wait(barrier, greeted)
+            pl.semaphore_signal(token, inc=1, device_id={"var": other}, device_id_type=MESH)
+
+        @pl.when(jnp.logical_not(mine))
+        def _():
+            pl.semaphore_wait(token, 1)
 
     lane = lax.broadcasted_iota(jnp.int32, (half * ny, nx), 1)
     backwards = nx - 1 - lax.broadcasted_iota(jnp.int32, (ny, nx), 1)
@@ -99,49 +109,50 @@
     def part(h):
         return pl.ds(h * chunk, chunk)
 
+    def go(condition, field, way, v, h, dst, rs, where):
+        @pl.when(condition)
+        def _():
+            rdma(rows_out.at[way, field, v, part(h)], dst, rows_ss.at[way], rs, where).start()
+
     def send_rows(field, v):
+        up_rs, down_rs = rows_rs.at[0, field, v], rows_rs.at[1, field, v]
         for h in (1, 0):
-            def go(condition, way, dst, rs, where, h=h):
-                @pl.when(condition)
-                def _():
-                    rdma(rows_out.at[field, way, v, part(h)], dst, rows_ss.at[field, way, v, h], rs, where).start()
-
-            up, down = rows_in.at[field, 0, v, part(h)], rows_in.at[field, 1, v, part(h)]
-            up_rs, down_rs = rows_rs.at[field, 0, v, h], rows_rs.at[field, 1, v, h]
-            below_top = jnp.logical_not(top)
-            off_bottom = jnp.logical_not(bottom)
-            if h == 1:
-                go(top & far, 0, fold.at[field, v], fold_rs.at[field, v], {"lat": lat - 2})
-            go(top & jnp.logical_not(far) if h == 1 else top, 0, down, down_rs, {"lon": mirror})
+            up, down = rows_in.at[0, field, v, part(h)], rows_in.at[1, field, v, part(h)]
+            below_top, above_bottom = off_top, off_bottom
             if h == 1 and relays:
                 odd = parity == 1
-                go(below_top & odd, 0, relay.at[field, v], relay_rs.at[field, v], {"lat": lat + 2})
-                go(off_bottom & jnp.logical_not(odd), 1, relay.at[field, v], relay_rs.at[field, v], {"lat": lat - 2})
+                go(top & far, field, 0, v, h, fold.at[field, v], fold_rs.at[field, v], {"lat": lat - 2})
+                go(below_top & odd, field, 0, v, h, relay.at[field, v], relay_rs.at[field, v], {"lat": lat + 2})
+                go(above_bottom & jnp.logical_not(odd), field, 1, v, h, relay.at[field, v], relay_rs.at[field, v],
+                   {"lat": lat - 2})
                 below_top = below_top & jnp.logical_not(odd)
-                off_bottom = off_bottom & odd
-            go(below_top, 0, up, up_rs, {"lat": lat + 1})
-            go(off_bottom, 1, down, down_rs, {"lat": lat - 1})
-
-    def any_rows(field, way, v, h):
-        return rdma(rows_out.at[field, way, v, part(h)], rows_in.at[field, way, v, part(h)],
-                    rows_ss.at[field, way, v, h], rows_rs.at[field, way, v, h], {"lon": east})
+                above_bottom = above_bottom & odd
+            go(below_top, field, 0, v, h, up, up_rs, {"lat": lat + 1})
+            go(above_bottom, field, 1, v, h, down, down_rs, {"lat": lat - 1})
+
+    def send_mirror(field, v):
+        for h in (1, 0):
+            go(top & jnp.logical_not(far) if h == 1 else top, field, 0, v, h, rows_in.at[1, field, v, part(h)],
+               rows_rs.at[1, field, v], {"lon": mirror})
+
+    def any_rows(field, way, v):
+        return rdma(rows_out.at[way, field, v], rows_in.at[way, field, v], rows_ss.at[way], rows_rs.at[way, field, v],
+                    {"lon": east})
 
     def relay_copy(field, v):
         way = 1 - parity
-        return rdma(relay.at[field, v], rows_in.at[field, way, v, part(1)], relay_ss.at[field, v],
-                    rows_rs.at[field, way, v, 1], {"lat": lat - step})
+        return rdma(relay.at[field, v], rows_in.at[way, field, v, part(1)], relay_ss.at[0], rows_rs.at[way, field, v],
+                    {"lat": lat - step})
 
     def relay_arrival(field, v):
-        return rdma(relay.at[field, v], relay.at[field, v], relay_ss.at[field, v], relay_rs.at[field, v],
-                    {"lon": east})
+        return rdma(relay.at[field, v], relay.at[field, v], relay_ss.at[0], relay_rs.at[field, v], {"lon": east})
 
     def fold_copy(field, v):
-        return rdma(fold.at[field, v], rows_in.at[field, 1, v, part(1)], fold_ss.at[field, v],
-                    rows_rs.at[field, 1, v, 1], {"lat": lat + 2, "lon": mirror})
+        return rdma(fold.at[field, v], rows_in.at[1, field, v, part(1)], fold_ss.at[0], rows_rs.at[1, field, v],
+                    {"lat": lat + 2, "lon": mirror})
 
     def fold_arrival(field, v):
-        return rdma(fold.at[field, v], fold.at[field, v], fold_ss.at[field, v], fold_rs.at[field, v],
-                    {"lon": east})
+        return rdma(fold.at[field, v], fold.at[field, v], fold_ss.at[0], fold_rs.at[field, v], {"lon": east})
 
     def pass_rows(field):
         if not relays:
@@ -160,18 +171,18 @@
 
     def pack_rows(field, v, planes):
         for z in range(nz):
-            rows_out[field, 1, v, z * radius:(z + 1) * radius] = planes[z][:radius]
+            rows_out[1, field, v, z * radius:(z + 1) * radius] = planes[z][:radius]
 
         @pl.when(top)
         def _():
             for z in range(nz):
                 turned = jnp.take_along_axis(planes[z], backwards, axis=1)
-                rows_out[field, 0, v, z * radius:(z + 1) * radius] = turned[ny - radius - 1:ny - 1]
+                rows_out[0, field, v, z * radius:(z + 1) * radius] = turned[ny - radius - 1:ny - 1]
 
         @pl.when(jnp.logical_not(top))
         def _():
             for z in range(nz):
-                rows_out[field, 0, v, z * radius:(z + 1) * radius] = planes[z][ny - radius:]
+                rows_out[0, field, v, z * radius:(z + 1) * radius] = planes[z][ny - radius:]
 
     def pack_lanes(field, flats):
         last = jnp.zeros((half * ny, nx), F32)
@@ -187,8 +198,11 @@
         lanes_out[field, 1] = first
 
     def lanes_copy(field, side):
-        return rdma(lanes_out.at[field, side], lanes_in.at[field, side], lanes_ss.at[field, side],
-                    lanes_rs.at[field, side], {"lon": east if side == 0 else west})
+        return rdma(lanes_out.at[field, side], lanes_in.at[field, side], lanes_ss.at[0], lanes_rs.at[field],
+                    {"lon": east if side == 0 else west})
+
+    def lanes_arrival(field):
+        return rdma(lanes_out.at[field], lanes_in.at[field], lanes_ss.at[0], lanes_rs.at[field], {"lon": east})
 
     def filter_x(field, v, flat):
         last, first = lanes_in[field, 0], lanes_in[field, 1]
@@ -209,8 +223,8 @@
             cols = slice(z * nx, (z + 1) * nx)
             part = slice(z * radius, (z + 1) * radius)
             pad[v, :ny, cols] = planes[z]
-            pad[v, ny:ny + radius, cols] = rows_in[field, 0, v, part]
-            pad[v, ny + radius:span, cols] = rows_in[field, 1, v, part]
+            pad[v, ny:ny + radius, cols] = rows_in[0, field, v, part]
+            pad[v, ny + radius:span, cols] = rows_in[1, field, v, part]
         high, low = halves(pad[v])
         both = dot(bands_y[v, :, :span], high)
         return both[:ny] + both[ny:] + dot(bands_y[v, :ny, :span], low)
@@ -226,12 +240,14 @@
 
     @pl.when(bottom)
     def _():
-        rows_in[:, 0] = jnp.zeros(rows_in.shape[:1] + rows_in.shape[2:], F32)
+        rows_in[0] = jnp.zeros(rows_in.shape[1:], F32)
 
     loads[0].wait()
     for v in range(nv):
         pack_rows(0, v, [con[v, z] for z in range(nz)])
     loads[1].wait()
+    for load in loads[4:]:
+        load.wait()
 
     @pl.when(upper)
     def _():
@@ -243,12 +259,9 @@
             col_out[0, b] = total
 
     def col_copy(which):
-        return rdma(col_out.at[which], col_in.at[which], col_ss.at[which], col_rs.at[which], {"var": other})
-
-    count = lambda condition: jnp.where(condition, 1, 0)
-    greeted = 4 + count(jnp.logical_not(bottom))
-    greeted = greeted + count(turning) + count(relaying) + count((top & far) | folding)
-    pl.semaphore_wait(barrier, greeted)
+        return rdma(col_out.at[which], col_in.at[which], col_ss.at[0], col_rs.at[0], {"var": other})
+
+    hear(jnp.logical_not(upper), greeted_lat)
 
     @pl.when(upper)
     def _():
@@ -278,8 +291,6 @@
 
     flats = [gra[v].reshape(nz * ny, nx) for v in range(nv)]
     pack_lanes(1, flats)
-    for side in range(2):
-        lanes_copy(1, side).start()
 
     circle = lax.broadcasted_iota(jnp.int32, (8, nx), 1)
     circle = jnp.minimum(circle, nx - circle)
@@ -306,23 +317,26 @@
         band = jnp.where(slot >= ny + radius, band * sign, band)
         bands_y[v, :ny], bands_y[v, ny:] = halves(band)
 
+    hear(upper, greeted_lon)
+    for side in range(2):
+        lanes_copy(1, side).start()
+    for v in range(nv):
+        send_mirror(0, v)
     pass_rows(0)
-    for side in range(2):
-        lanes_copy(1, side).wait_recv()
+    lanes_arrival(1).wait_recv()
     for v in range(nv):
         flat = filter_x(1, v, gra[v].reshape(nz * ny, nx))
         gra[v] = flat.reshape(nz, ny, nx)
         pack_rows(1, v, [flat[z * ny:(z + 1) * ny] for z in range(nz)])
         send_rows(1, v)
+        send_mirror(1, v)
 
     def wait_rows(field, v):
-        for h in range(2):
-            any_rows(field, 1, v, h).wait_recv()
-
-        @pl.when(jnp.logical_not(bottom))
-        def _():
-            for h in range(2):
-                any_rows(field, 0, v, h).wait_recv()
+        any_rows(field, 1, v).wait_recv()
+
+        @pl.when(off_bottom)
+        def _():
+            any_rows(field, 0, v).wait_recv()
 
     flats = []
     for v in range(nv):
@@ -334,8 +348,7 @@
     for side in range(2):
         lanes_copy(0, side).start()
     pass_rows(1)
-    for side in range(2):
-        lanes_copy(0, side).wait_recv()
+    lanes_arrival(0).wait_recv()
     for v in range(nv):
         flat = filter_x(0, v, con[v].reshape(nz * ny, nx))
         levels = filter_z(v, [flat[z * ny:(z + 1) * ny] for z in range(nz)])
@@ -367,32 +380,27 @@
                 for b in range(nv):
                     total = total + bal[a, b, z] * col_in[1, b]
                 inc_ref[a, z] = total
-        col_copy(0).wait_send()
-
-    @pl.when(jnp.logical_not(upper))
-    def _():
-        col_copy(1).wait_send()
-
-    for field in range(2):
-        for side in range(2):
-            lanes_copy(field, side).wait_send()
-        for v in range(nv):
-            for h in range(2):
-                any_rows(field, 0, v, h).wait_send()
-
-            @pl.when(jnp.logical_not(bottom))
-            def _():
-                for h in range(2):
-                    any_rows(field, 1, v, h).wait_send()
-
-            if relays:
-                @pl.when(relaying)
-                def _():
-                    relay_copy(field, v).wait_send()
-
-                @pl.when(folding)
-                def _():
-                    fold_copy(field, v).wait_send()
+
+    def drain(src, dst, sem, condition):
+        @pl.when(condition)
+        def _():
+            rdma(src, dst, sem, sem, {"lon": east}).wait_send()
+
+    col_copy(0).wait_send()
+    rdma(lanes_out, lanes_in, lanes_ss.at[0], lanes_rs.at[0], {"lon": east}).wait_send()
+    drain(rows_out.at[0], rows_in.at[0], rows_ss.at[0], lat >= 0)
+    drain(rows_out.at[1], rows_in.at[1], rows_ss.at[1], off_bottom)
+    if relays:
+        drain(relay, relay, relay_ss.at[0], relaying)
+        drain(fold, fold, fold_ss.at[0], folding)
+
+
+def store(inc, cg, inc_out, cg_out, sems):
+    copies = [pltpu.make_async_copy(src, dst, sems.at[i]) for i, (src, dst) in enumerate(((inc, inc_out), (cg, cg_out)))]
+    for copy in copies:
+        copy.start()
+    for copy in copies:
+        copy.wait()
 
 
 def per_device(lats, lons, control, gradient, std_dev, sea_mask, x_taps, y_taps, z_taps, column_weight, balance):
@@ -400,15 +408,14 @@
     radius = x_taps.shape[1] - 1
     span = ny + 2 * radius
     anywhere = pl.BlockSpec(memory_space=pl.ANY)
-    scalars = pl.BlockSpec(memory_space=pltpu.SMEM)
     vmem = pl.BlockSpec(memory_space=pltpu.VMEM)
     dma = pltpu.SemaphoreType.DMA
-    return pl.pallas_call(
+    outs = pl.pallas_call(
         functools.partial(kernel, (lats, lons, radius)),
         out_shape=(pltpu.VMEM(control.shape, F32),) * 2,
-        in_specs=[anywhere] * 4 + [scalars] * 5,
+        in_specs=[anywhere] * 9,
         out_specs=(vmem, vmem),
-        scratch_shapes=[
+        scratch_shapes=[pltpu.SMEM(a.shape, F32) for a in (x_taps, y_taps, z_taps, column_weight, balance)] + [
             pltpu.VMEM(control.shape, F32),
             pltpu.VMEM(control.shape, F32),
             pltpu.VMEM(std_dev.shape, F32),
@@ -424,20 +431,29 @@
             pltpu.VMEM((2, nv, ny, nx), F32),
             pltpu.VMEM((2, nv, nz * radius // 2, nx), F32),
             pltpu.VMEM((2, nv, nz * radius // 2, nx), F32),
-            dma((4,)),
-            dma((2, 2, nv, 2)),
-            dma((2, 2, nv, 2)),
+            dma((9,)),
+            dma((2,)),
+            dma((2, 2, nv)),
+            dma((1,)),
             dma((2, nv)),
+            dma((1,)),
             dma((2, nv)),
-            dma((2, nv)),
-            dma((2, nv)),
-            dma((2, 2)),
-            dma((2, 2)),
+            dma((1,)),
             dma((2,)),
-            dma((2,)),
+            dma((1,)),
+            dma((1,)),
+            pltpu.SemaphoreType.REGULAR,
         ],
         compiler_params=pltpu.CompilerParams(collective_id=0, has_side_effects=True),
     )(control, gradient, std_dev, sea_mask, x_taps, y_taps, z_taps, column_weight, balance)
+    return pl.pallas_call(
+        store,
+        out_shape=(jax.ShapeDtypeStruct(control.shape, F32),) * 2,
+        in_specs=[anywhere] * 2,
+        out_specs=(anywhere,) * 2,
+        scratch_shapes=[dma((2,))],
+        compiler_params=pltpu.CompilerParams(vmem_limit_bytes=1 << 20),
+    )(*outs)
 
 
 def solution(mesh):

time: 21.1 us -> 18.9 us (0.90)
  the two profiles are of different devices: /device:TPU:7 before, /device:TPU:0 now
where the time goes in v1:
time: 18.9 us; the launch traced here: 18.6 us
  Pallas kernels  18 us (95%)
  between operations  0.64 us (3%)
    pallas_call x1, Pallas kernels, per_device(): pl.pallas_call(functools.partial(kernel, (lats, lons, radius)), out_shape...  17.2 us
    pallas_call x1, Pallas kernels, per_device(): pl.pallas_call(store, out_shape=(jax.ShapeDtypeStruct(control.shape, F32)...  0.76 us

profile of v1, /device:TPU:0, one launch (start us, length us, event | category | flops | bytes accessed | tf_op | source)
XLA Modules:
  0.0 18.6 jit_solution(13071966992144123347)
XLA Ops:
  0.6 17.2 %shard_map.104 = (f32[3,4,32,128]{3,2,1,0:T(8,128)S(1)}, f32[3,4,32,128]{3,2,1,0:T(8,128)S(1)}) custom-call(f32[3,4,32,128]{3,2,1,0:T(8,128)} %control_hbm.1, f32[3,4,32,128]{3,2,1,0:T(8,128)} %gradient_hbm.1, f32[3,32,128]{2,1,0:T(8,128)} %std_hbm.1, s32[32,128]{1,0:T(8,128)} %mask_hbm.1, f32[3,21]{1,0:T(4,128)} %xt_hbm.1, f32[3,21]{1,0:T(4,128)} %yt_hbm.1, ...), custom_call_target="tpu_custom_call" | custom-call | tf_op jit(solution)/shard_map/pallas_call | solution.py:413
  17.9 0.8 %shard_map.105 = (f32[3,4,32,128]{3,2,1,0:T(8,128)}, f32[3,4,32,128]{3,2,1,0:T(8,128)}) custom-call(f32[3,4,32,128]{3,2,1,0:T(8,128)S(1)} %get-tuple-element.4.inc, f32[3,4,32,128]{3,2,1,0:T(8,128)S(1)} %get-tuple-element.5.cg), custom_call_target="tpu_custom_call" | custom-call | tf_op jit(solution)/shard_map/pallas_call | solution.py:449

commit v2 on v1

--- a/solution.py
+++ b/solution.py
@@ -32,9 +32,9 @@
     sizes,
     control_hbm, gradient_hbm, std_hbm, mask_hbm, xt_hbm, yt_hbm, zt_hbm, cw_hbm, bal_hbm,
     inc_ref, cg_ref,
-    xt, yt, zt, cw, bal, con, gra, std, mask, bands_x, bands_y, rows_out, rows_in, lanes_out, lanes_in,
+    xt, yt, zt, cw, bal, con, gra, std, mask, bands_x, bands_y, rows_out, rows_in, lanes_out, lanes_in, strips_out, strips_in,
     pad, col_out, col_in,
-    relay, fold, load_sem, rows_ss, rows_rs, relay_ss, relay_rs, fold_ss, fold_rs, lanes_ss, lanes_rs, col_ss, col_rs, token,
+    relay, fold, load_sem, rows_ss, rows_rs, relay_ss, relay_rs, fold_ss, fold_rs, lanes_ss, lanes_rs, col_ss, col_rs, token, mirrored,
 ):
     lats, lons, radius = sizes
     nv, nz, ny, nx = con.shape
@@ -80,26 +80,24 @@
         def _():
             pl.semaphore_signal(barrier, inc=1, device_id=where, device_id_type=MESH)
 
-    greet(off_top, {"lat": lat + 1, "var": 0})
-    greet(off_bottom, {"lat": lat - 1, "var": 0})
-    greet(turning, {"lat": ahead, "var": 0})
-    greet(relaying, {"lat": behind, "var": 0})
-    pl.semaphore_signal(barrier, inc=1, device_id={"lon": east, "var": 1}, device_id_type=MESH)
-    pl.semaphore_signal(barrier, inc=1, device_id={"lon": west, "var": 1}, device_id_type=MESH)
-    greet(top, {"lon": mirror, "var": 1})
-    greet(top & far, {"lat": lat - 2, "lon": mirror, "var": 1})
-    greet(folding, {"lat": lat + 2, "lon": mirror, "var": 1})
+    greet(off_top, {"lat": lat + 1, "var": 1})
+    greet(off_bottom, {"lat": lat - 1, "var": 1})
+    greet(turning, {"lat": ahead, "var": 1})
+    greet(relaying, {"lat": behind, "var": 1})
+    pl.semaphore_signal(barrier, inc=1, device_id={"lon": east, "var": 0}, device_id_type=MESH)
+    pl.semaphore_signal(barrier, inc=1, device_id={"lon": west, "var": 0}, device_id_type=MESH)
+    greet(top, {"lon": mirror, "var": 0})
     count = lambda condition: jnp.where(condition, 1, 0)
     greeted_lat = 1 + 2 * (count(off_top) + count(off_bottom) + count(turning) + count(relaying))
-    greeted_lon = 5 + 2 * (count(top) + count((top & far) | folding))
-
-    def hear(mine, greeted):
-        @pl.when(mine)
+    greeted_lon = 5 + 2 * count(top)
+
+    def hear(condition, mine, greeted):
+        @pl.when(condition & mine)
         def _():
             pl.semaphore_wait(barrier, greeted)
             pl.semaphore_signal(token, inc=1, device_id={"var": other}, device_id_type=MESH)
 
-        @pl.when(jnp.logical_not(mine))
+        @pl.when(condition & jnp.logical_not(mine))
         def _():
             pl.semaphore_wait(token, 1)
 
@@ -165,6 +163,8 @@
 
         @pl.when(folding)
         def _():
+            if field == 0:
+                pl.semaphore_wait(mirrored, 1)
             for v in range(nv):
                 fold_arrival(field, v).wait_recv()
                 fold_copy(field, v).start()
@@ -184,7 +184,7 @@
             for z in range(nz):
                 rows_out[0, field, v, z * radius:(z + 1) * radius] = planes[z][ny - radius:]
 
-    def pack_lanes(field, flats):
+    def pack_lanes(flats):
         last = jnp.zeros((half * ny, nx), F32)
         first = jnp.zeros((half * ny, nx), F32)
         for h in range(2):
@@ -194,24 +194,58 @@
                 block = flats[v][h * half * ny:(h + 1) * half * ny]
                 last = jnp.where(inside, pltpu.roll(block, (start - (nx - radius)) % nx, 1), last)
                 first = jnp.where(inside, pltpu.roll(block, start, 1) if start else block, first)
-        lanes_out[field, 0] = last
-        lanes_out[field, 1] = first
-
-    def lanes_copy(field, side):
-        return rdma(lanes_out.at[field, side], lanes_in.at[field, side], lanes_ss.at[0], lanes_rs.at[field],
+        lanes_out[0] = last
+        lanes_out[1] = first
+
+    def pack_strip(v, planes):
+        last = jnp.zeros((ny, nx), F32)
+        first = jnp.zeros((ny, nx), F32)
+        for z in range(nz):
+            start = z * radius
+            inside = (lane[:ny] >= start) & (lane[:ny] < start + radius)
+            last = jnp.where(inside, pltpu.roll(planes[z], (start - (nx - radius)) % nx, 1), last)
+            first = jnp.where(inside, pltpu.roll(planes[z], start, 1) if start else planes[z], first)
+        strips_out[v, 0] = last
+        strips_out[v, 1] = first
+
+    def lanes_copy(side):
+        return rdma(lanes_out.at[side], lanes_in.at[side], lanes_ss.at[0], lanes_rs.at[0],
                     {"lon": east if side == 0 else west})
 
-    def lanes_arrival(field):
-        return rdma(lanes_out.at[field], lanes_in.at[field], lanes_ss.at[0], lanes_rs.at[field], {"lon": east})
-
-    def filter_x(field, v, flat):
-        last, first = lanes_in[field, 0], lanes_in[field, 1]
-        wraps = []
-        for h in range(2):
-            start = (h * nv + v) * radius
-            from_west = pltpu.roll(last, (nx - radius - start) % nx, 1)
-            from_east = pltpu.roll(first, (-start) % nx, 1) if start else first
-            wraps.append(jnp.where(lane >= nx - radius, from_west, jnp.where(lane < radius, from_east, 0.0)))
+    def strip_copy(v, side):
+        return rdma(strips_out.at[v, side], strips_in.at[v, side], lanes_ss.at[1], lanes_rs.at[1 + v],
+                    {"lon": east if side == 0 else west})
+
+    def send_sides(copy):
+        @pl.when(2 * lon < lons)
+        def _():
+            for side in (1, 0):
+                copy(side).start()
+
+        @pl.when(2 * lon >= lons)
+        def _():
+            for side in (0, 1):
+                copy(side).start()
+
+    def lanes_arrival():
+        return rdma(lanes_out, lanes_in, lanes_ss.at[0], lanes_rs.at[0], {"lon": east})
+
+    def strip_arrival(v):
+        return rdma(strips_out.at[v], strips_in.at[v], lanes_ss.at[1], lanes_rs.at[1 + v], {"lon": east})
+
+    def wrapped(rows, last, first, start):
+        from_west = pltpu.roll(last, (nx - radius - start) % nx, 1)
+        from_east = pltpu.roll(first, (-start) % nx, 1) if start else first
+        spot = lane[:rows]
+        return jnp.where(spot >= nx - radius, from_west, jnp.where(spot < radius, from_east, 0.0))
+
+    def lanes_wraps(v):
+        return [wrapped(half * ny, lanes_in[0], lanes_in[1], (h * nv + v) * radius) for h in range(2)]
+
+    def strip_wraps(v):
+        return [wrapped(ny, strips_in[v, 0], strips_in[v, 1], z * radius) for z in range(nz)]
+
+    def filter_x(v, flat, wraps):
         high, low = halves(jnp.concatenate([flat, jnp.concatenate(wraps, axis=0)], axis=1))
         both = dot(high, bands_x[v])
         return both[:, :nx] + both[:, nx:] + dot(low, bands_x[v, :, :nx])
@@ -261,7 +295,7 @@
     def col_copy(which):
         return rdma(col_out.at[which], col_in.at[which], col_ss.at[0], col_rs.at[0], {"var": other})
 
-    hear(jnp.logical_not(upper), greeted_lat)
+    hear(lat >= 0, upper, greeted_lat)
 
     @pl.when(upper)
     def _():
@@ -275,6 +309,8 @@
     sea = mask[...].astype(F32)
     for v in range(nv):
         std[v] = std[v] * sea
+
+    hear((lon > 0) & jnp.logical_not(upper), jnp.logical_not(upper), greeted_lon)
 
     @pl.when(upper)
     def _():
@@ -290,7 +326,17 @@
                 gra[v, z] = (gra[v, z] + cw[v, z] * col_in[0, v]) * std[v]
 
     flats = [gra[v].reshape(nz * ny, nx) for v in range(nv)]
-    pack_lanes(1, flats)
+    pack_lanes(flats)
+
+    hear((lon == 0) | upper, jnp.logical_not(upper), greeted_lon)
+    send_sides(lanes_copy)
+
+    @pl.when(top & far)
+    def _():
+        pl.semaphore_signal(mirrored, inc=1, device_id={"lat": lat - 2}, device_id_type=MESH)
+
+    for v in range(nv):
+        send_mirror(0, v)
 
     circle = lax.broadcasted_iota(jnp.int32, (8, nx), 1)
     circle = jnp.minimum(circle, nx - circle)
@@ -317,15 +363,10 @@
         band = jnp.where(slot >= ny + radius, band * sign, band)
         bands_y[v, :ny], bands_y[v, ny:] = halves(band)
 
-    hear(upper, greeted_lon)
-    for side in range(2):
-        lanes_copy(1, side).start()
-    for v in range(nv):
-        send_mirror(0, v)
     pass_rows(0)
-    lanes_arrival(1).wait_recv()
-    for v in range(nv):
-        flat = filter_x(1, v, gra[v].reshape(nz * ny, nx))
+    lanes_arrival().wait_recv()
+    for v in range(nv):
+        flat = filter_x(v, gra[v].reshape(nz * ny, nx), lanes_wraps(v))
         gra[v] = flat.reshape(nz, ny, nx)
         pack_rows(1, v, [flat[z * ny:(z + 1) * ny] for z in range(nz)])
         send_rows(1, v)
@@ -338,19 +379,18 @@
         def _():
             any_rows(field, 0, v).wait_recv()
 
-    flats = []
     for v in range(nv):
         wait_rows(0, v)
         out = filter_y(0, v, [con[v, z] for z in range(nz)])
-        for z in range(nz):
-            con[v, z] = out[:, z * nx:(z + 1) * nx]
-    pack_lanes(0, [con[v].reshape(nz * ny, nx) for v in range(nv)])
-    for side in range(2):
-        lanes_copy(0, side).start()
+        planes = [out[:, z * nx:(z + 1) * nx] for z in range(nz)]
+        for z in range(nz):
+            con[v, z] = planes[z]
+        pack_strip(v, planes)
+        send_sides(functools.partial(strip_copy, v))
     pass_rows(1)
-    lanes_arrival(0).wait_recv()
-    for v in range(nv):
-        flat = filter_x(0, v, con[v].reshape(nz * ny, nx))
+    for v in range(nv):
+        strip_arrival(v).wait_recv()
+        flat = filter_x(v, con[v].reshape(nz * ny, nx), strip_wraps(v))
         levels = filter_z(v, [flat[z * ny:(z + 1) * ny] for z in range(nz)])
         total = jnp.zeros((ny, nx), F32)
         for z in range(nz):
@@ -387,7 +427,8 @@
             rdma(src, dst, sem, sem, {"lon": east}).wait_send()
 
     col_copy(0).wait_send()
-    rdma(lanes_out, lanes_in, lanes_ss.at[0], lanes_rs.at[0], {"lon": east}).wait_send()
+    lanes_arrival().wait_send()
+    rdma(strips_out, strips_in, lanes_ss.at[1], lanes_rs.at[1], {"lon": east}).wait_send()
     drain(rows_out.at[0], rows_in.at[0], rows_ss.at[0], lat >= 0)
     drain(rows_out.at[1], rows_in.at[1], rows_ss.at[1], off_bottom)
     if relays:
@@ -424,8 +465,10 @@
             pltpu.VMEM((nv, 2 * ny, nx), BF16),
             pltpu.VMEM((2, 2, nv, nz * radius, nx), F32),
             pltpu.VMEM((2, 2, nv, nz * radius, nx), F32),
-            pltpu.VMEM((2, 2, nz // 2 * ny, nx), F32),
-            pltpu.VMEM((2, 2, nz // 2 * ny, nx), F32),
+            pltpu.VMEM((2, nz // 2 * ny, nx), F32),
+            pltpu.VMEM((2, nz // 2 * ny, nx), F32),
+            pltpu.VMEM((nv, 2, ny, nx), F32),
+            pltpu.VMEM((nv, 2, ny, nx), F32),
             pltpu.VMEM((nv, span, nz * nx), F32),
             pltpu.VMEM((2, nv, ny, nx), F32),
             pltpu.VMEM((2, nv, ny, nx), F32),
@@ -438,10 +481,11 @@
             dma((2, nv)),
             dma((1,)),
             dma((2, nv)),
-            dma((1,)),
             dma((2,)),
+            dma((1 + nv,)),
             dma((1,)),
             dma((1,)),
+            pltpu.SemaphoreType.REGULAR,
             pltpu.SemaphoreType.REGULAR,
         ],
         compiler_params=pltpu.CompilerParams(collective_id=0, has_side_effects=True),

time: 18.9 us -> 18.2 us (0.963)
  Pallas kernels: 18 us -> 17.4 us
    pallas_call x1, Pallas kernels: 17.2 us -> 16.6 us  [per_device(): pl.pallas_call(functools.partial(kernel, (lats, lons, radius)), out_shape...]
where the time goes in v2:
time: 18.2 us; the launch traced here: 18 us
  Pallas kernels  17.4 us (96%)
  between operations  0.64 us (4%)
    pallas_call x1, Pallas kernels, per_device(): pl.pallas_call(functools.partial(kernel, (lats, lons, radius)), out_shape...  16.6 us
    pallas_call x1, Pallas kernels, per_device(): pl.pallas_call(store, out_shape=(jax.ShapeDtypeStruct(control.shape, F32)...  0.76 us

profile of v2, /device:TPU:0, one launch (start us, length us, event | category | flops | bytes accessed | tf_op | source)
XLA Modules:
  0.0 18.0 jit_solution(9283626372296281211)
XLA Ops:
  0.6 16.6 %shard_map.104 = (f32[3,4,32,128]{3,2,1,0:T(8,128)S(1)}, f32[3,4,32,128]{3,2,1,0:T(8,128)S(1)}) custom-call(f32[3,4,32,128]{3,2,1,0:T(8,128)} %control_hbm.1, f32[3,4,32,128]{3,2,1,0:T(8,128)} %gradient_hbm.1, f32[3,32,128]{2,1,0:T(8,128)} %std_hbm.1, s32[32,128]{1,0:T(8,128)} %mask_hbm.1, f32[3,21]{1,0:T(4,128)} %xt_hbm.1, f32[3,21]{1,0:T(4,128)} %yt_hbm.1, ...), custom_call_target="tpu_custom_call" | custom-call | tf_op jit(solution)/shard_map/pallas_call | solution.py:454
  17.2 0.8 %shard_map.105 = (f32[3,4,32,128]{3,2,1,0:T(8,128)}, f32[3,4,32,128]{3,2,1,0:T(8,128)}) custom-call(f32[3,4,32,128]{3,2,1,0:T(8,128)S(1)} %get-tuple-element.4.inc, f32[3,4,32,128]{3,2,1,0:T(8,128)S(1)} %get-tuple-element.5.cg), custom_call_target="tpu_custom_call" | custom-call | tf_op jit(solution)/shard_map/pallas_call | solution.py:493

commit v3 on v2

--- a/solution.py
+++ b/solution.py
@@ -34,7 +34,7 @@
     inc_ref, cg_ref,
     xt, yt, zt, cw, bal, con, gra, std, mask, bands_x, bands_y, rows_out, rows_in, lanes_out, lanes_in, strips_out, strips_in,
     pad, col_out, col_in,
-    relay, fold, load_sem, rows_ss, rows_rs, relay_ss, relay_rs, fold_ss, fold_rs, lanes_ss, lanes_rs, col_ss, col_rs, token, mirrored,
+    relay, fold, fold_inner, load_sem, rows_ss, rows_rs, relay_ss, relay_rs, fold_ss, fold_rs, lanes_ss, lanes_rs, col_ss, col_rs, token, mirrored,
 ):
     lats, lons, radius = sizes
     nv, nz, ny, nx = con.shape
@@ -51,6 +51,7 @@
     turning = (ahead >= 0) & (ahead < lats) & relays
     relaying = (behind >= 0) & (behind < lats) & relays
     far = (mirror != lon) & relays
+    inner = far & (2 * jnp.abs(lons - 1 - 2 * lon) < lons)
     folding = far & (lat == lats - 3)
     chunk = nz * radius // 2
 
@@ -107,31 +108,41 @@
     def part(h):
         return pl.ds(h * chunk, chunk)
 
-    def go(condition, field, way, v, h, dst, rs, where):
+    def go(condition, field, way, v, piece, dst, rs, where):
         @pl.when(condition)
         def _():
-            rdma(rows_out.at[way, field, v, part(h)], dst, rows_ss.at[way], rs, where).start()
+            rdma(rows_out.at[way, field, v, piece], dst, rows_ss.at[way], rs, where).start()
+
+    def straight(condition, field, way, v, piece, where):
+        go(condition, field, way, v, piece, rows_in.at[way, field, v, piece], rows_rs.at[way, field, v], where)
+
+    odd, even, whole = parity == 1, parity == 0, pl.ds(0, 2 * chunk)
 
     def send_rows(field, v):
-        up_rs, down_rs = rows_rs.at[0, field, v], rows_rs.at[1, field, v]
-        for h in (1, 0):
-            up, down = rows_in.at[0, field, v, part(h)], rows_in.at[1, field, v, part(h)]
-            below_top, above_bottom = off_top, off_bottom
-            if h == 1 and relays:
-                odd = parity == 1
-                go(top & far, field, 0, v, h, fold.at[field, v], fold_rs.at[field, v], {"lat": lat - 2})
-                go(below_top & odd, field, 0, v, h, relay.at[field, v], relay_rs.at[field, v], {"lat": lat + 2})
-                go(above_bottom & jnp.logical_not(odd), field, 1, v, h, relay.at[field, v], relay_rs.at[field, v],
-                   {"lat": lat - 2})
-                below_top = below_top & jnp.logical_not(odd)
-                above_bottom = above_bottom & odd
-            go(below_top, field, 0, v, h, up, up_rs, {"lat": lat + 1})
-            go(above_bottom, field, 1, v, h, down, down_rs, {"lat": lat - 1})
+        if relays:
+            if field == 0:
+                go(top & far, 0, 0, v, part(1), fold.at[v], fold_rs.at[0, v], {"lat": lat - 2})
+            else:
+                go(top & inner, 1, 0, v, whole, fold_inner.at[v], fold_rs.at[1, v], {"lat": lat - 2})
+            go(off_top & odd, field, 0, v, part(1), relay.at[field, v], relay_rs.at[field, v], {"lat": lat + 2})
+            go(off_bottom & even, field, 1, v, part(1), relay.at[field, v], relay_rs.at[field, v], {"lat": lat - 2})
+        straight(off_top & even if relays else off_top, field, 0, v, whole, {"lat": lat + 1})
+        straight(off_bottom & odd if relays else off_bottom, field, 1, v, whole, {"lat": lat - 1})
+
+    def send_across(field, v):
+        if relays:
+            straight(off_top & odd, field, 0, v, part(0), {"lat": lat + 1})
+            straight(off_bottom & even, field, 1, v, part(0), {"lat": lat - 1})
 
     def send_mirror(field, v):
-        for h in (1, 0):
-            go(top & jnp.logical_not(far) if h == 1 else top, field, 0, v, h, rows_in.at[1, field, v, part(h)],
-               rows_rs.at[1, field, v], {"lon": mirror})
+        def direct(condition, piece):
+            go(condition, field, 0, v, piece, rows_in.at[1, field, v, piece], rows_rs.at[1, field, v], {"lon": mirror})
+
+        if field == 0:
+            direct(top & jnp.logical_not(far), part(1))
+            direct(top, part(0))
+        else:
+            direct(top & jnp.logical_not(inner), whole)
 
     def any_rows(field, way, v):
         return rdma(rows_out.at[way, field, v], rows_in.at[way, field, v], rows_ss.at[way], rows_rs.at[way, field, v],
@@ -146,11 +157,13 @@
         return rdma(relay.at[field, v], relay.at[field, v], relay_ss.at[0], relay_rs.at[field, v], {"lon": east})
 
     def fold_copy(field, v):
-        return rdma(fold.at[field, v], rows_in.at[1, field, v, part(1)], fold_ss.at[0], rows_rs.at[1, field, v],
+        src, piece = (fold.at[v], part(1)) if field == 0 else (fold_inner.at[v], whole)
+        return rdma(src, rows_in.at[1, field, v, piece], fold_ss.at[field], rows_rs.at[1, field, v],
                     {"lat": lat + 2, "lon": mirror})
 
     def fold_arrival(field, v):
-        return rdma(fold.at[field, v], fold.at[field, v], fold_ss.at[0], fold_rs.at[field, v], {"lon": east})
+        landed = fold.at[v] if field == 0 else fold_inner.at[v]
+        return rdma(landed, landed, fold_ss.at[field], fold_rs.at[field, v], {"lon": east})
 
     def pass_rows(field):
         if not relays:
@@ -161,7 +174,7 @@
                 relay_arrival(field, v).wait_recv()
                 relay_copy(field, v).start()
 
-        @pl.when(folding)
+        @pl.when(folding if field == 0 else folding & inner)
         def _():
             if field == 0:
                 pl.semaphore_wait(mirrored, 1)
@@ -197,23 +210,26 @@
         lanes_out[0] = last
         lanes_out[1] = first
 
-    def pack_strip(v, planes):
+    group = nv * nz // 2
+
+    def pack_strip(g, planes):
         last = jnp.zeros((ny, nx), F32)
         first = jnp.zeros((ny, nx), F32)
-        for z in range(nz):
-            start = z * radius
+        for p in range(group):
+            start = p * radius
             inside = (lane[:ny] >= start) & (lane[:ny] < start + radius)
-            last = jnp.where(inside, pltpu.roll(planes[z], (start - (nx - radius)) % nx, 1), last)
-            first = jnp.where(inside, pltpu.roll(planes[z], start, 1) if start else planes[z], first)
-        strips_out[v, 0] = last
-        strips_out[v, 1] = first
+            plane = planes[g * group + p]
+            last = jnp.where(inside, pltpu.roll(plane, (start - (nx - radius)) % nx, 1), last)
+            first = jnp.where(inside, pltpu.roll(plane, start, 1) if start else plane, first)
+        strips_out[g, 0] = last
+        strips_out[g, 1] = first
 
     def lanes_copy(side):
         return rdma(lanes_out.at[side], lanes_in.at[side], lanes_ss.at[0], lanes_rs.at[0],
                     {"lon": east if side == 0 else west})
 
-    def strip_copy(v, side):
-        return rdma(strips_out.at[v, side], strips_in.at[v, side], lanes_ss.at[1], lanes_rs.at[1 + v],
+    def strip_copy(g, side):
+        return rdma(strips_out.at[g, side], strips_in.at[g, side], lanes_ss.at[1], lanes_rs.at[1 + g],
                     {"lon": east if side == 0 else west})
 
     def send_sides(copy):
@@ -230,8 +246,8 @@
     def lanes_arrival():
         return rdma(lanes_out, lanes_in, lanes_ss.at[0], lanes_rs.at[0], {"lon": east})
 
-    def strip_arrival(v):
-        return rdma(strips_out.at[v], strips_in.at[v], lanes_ss.at[1], lanes_rs.at[1 + v], {"lon": east})
+    def strip_arrival(g):
+        return rdma(strips_out.at[g], strips_in.at[g], lanes_ss.at[1], lanes_rs.at[1 + g], {"lon": east})
 
     def wrapped(rows, last, first, start):
         from_west = pltpu.roll(last, (nx - radius - start) % nx, 1)
@@ -243,7 +259,8 @@
         return [wrapped(half * ny, lanes_in[0], lanes_in[1], (h * nv + v) * radius) for h in range(2)]
 
     def strip_wraps(v):
-        return [wrapped(ny, strips_in[v, 0], strips_in[v, 1], z * radius) for z in range(nz)]
+        spots = [divmod(v * nz + z, group) for z in range(nz)]
+        return [wrapped(ny, strips_in[g, 0], strips_in[g, 1], p * radius) for g, p in spots]
 
     def filter_x(v, flat, wraps):
         high, low = halves(jnp.concatenate([flat, jnp.concatenate(wraps, axis=0)], axis=1))
@@ -335,6 +352,8 @@
     def _():
         pl.semaphore_signal(mirrored, inc=1, device_id={"lat": lat - 2}, device_id_type=MESH)
 
+    for v in range(nv):
+        send_across(0, v)
     for v in range(nv):
         send_mirror(0, v)
 
@@ -370,7 +389,10 @@
         gra[v] = flat.reshape(nz, ny, nx)
         pack_rows(1, v, [flat[z * ny:(z + 1) * ny] for z in range(nz)])
         send_rows(1, v)
-        send_mirror(1, v)
+        if v == 0:
+            send_mirror(1, v)
+    for v in range(nv):
+        send_across(1, v)
 
     def wait_rows(field, v):
         any_rows(field, 1, v).wait_recv()
@@ -379,17 +401,24 @@
         def _():
             any_rows(field, 0, v).wait_recv()
 
+    planes = []
     for v in range(nv):
         wait_rows(0, v)
         out = filter_y(0, v, [con[v, z] for z in range(nz)])
-        planes = [out[:, z * nx:(z + 1) * nx] for z in range(nz)]
         for z in range(nz):
-            con[v, z] = planes[z]
-        pack_strip(v, planes)
-        send_sides(functools.partial(strip_copy, v))
+            con[v, z] = out[:, z * nx:(z + 1) * nx]
+            planes.append(con[v, z])
+            if len(planes) % group == 0:
+                pack_strip(len(planes) // group - 1, planes)
+                send_sides(functools.partial(strip_copy, len(planes) // group - 1))
+    for v in range(1, nv):
+        send_mirror(1, v)
     pass_rows(1)
-    for v in range(nv):
-        strip_arrival(v).wait_recv()
+    heard = 0
+    for v in range(nv):
+        while heard * group < (v + 1) * nz:
+            strip_arrival(heard).wait_recv()
+            heard += 1
         flat = filter_x(v, con[v].reshape(nz * ny, nx), strip_wraps(v))
         levels = filter_z(v, [flat[z * ny:(z + 1) * ny] for z in range(nz)])
         total = jnp.zeros((ny, nx), F32)
@@ -434,6 +463,7 @@
     if relays:
         drain(relay, relay, relay_ss.at[0], relaying)
         drain(fold, fold, fold_ss.at[0], folding)
+        drain(fold_inner, fold_inner, fold_ss.at[1], folding & inner)
 
 
 def store(inc, cg, inc_out, cg_out, sems):
@@ -467,22 +497,23 @@
             pltpu.VMEM((2, 2, nv, nz * radius, nx), F32),
             pltpu.VMEM((2, nz // 2 * ny, nx), F32),
             pltpu.VMEM((2, nz // 2 * ny, nx), F32),
-            pltpu.VMEM((nv, 2, ny, nx), F32),
-            pltpu.VMEM((nv, 2, ny, nx), F32),
+            pltpu.VMEM((2, 2, ny, nx), F32),
+            pltpu.VMEM((2, 2, ny, nx), F32),
             pltpu.VMEM((nv, span, nz * nx), F32),
             pltpu.VMEM((2, nv, ny, nx), F32),
             pltpu.VMEM((2, nv, ny, nx), F32),
             pltpu.VMEM((2, nv, nz * radius // 2, nx), F32),
-            pltpu.VMEM((2, nv, nz * radius // 2, nx), F32),
+            pltpu.VMEM((nv, nz * radius // 2, nx), F32),
+            pltpu.VMEM((nv, nz * radius, nx), F32),
             dma((9,)),
             dma((2,)),
             dma((2, 2, nv)),
             dma((1,)),
             dma((2, nv)),
-            dma((1,)),
+            dma((2,)),
             dma((2, nv)),
             dma((2,)),
-            dma((1 + nv,)),
+            dma((3,)),
             dma((1,)),
             dma((1,)),
             pltpu.SemaphoreType.REGULAR,

time: 18.2 us -> 17.9 us (0.984)
  Pallas kernels: 17.4 us -> 16.9 us
    pallas_call x1, Pallas kernels: 16.6 us -> 16.2 us  [per_device(): pl.pallas_call(functools.partial(kernel, (lats, lons, radius)), out_shape...]
where the time goes in v3:
time: 17.9 us; the launch traced here: 17.6 us
  Pallas kernels  16.9 us (94%)
  between operations  0.64 us (4%)
    pallas_call x1, Pallas kernels, per_device(): pl.pallas_call(functools.partial(kernel, (lats, lons, radius)), out_shape...  16.2 us
    pallas_call x1, Pallas kernels, per_device(): pl.pallas_call(store, out_shape=(jax.ShapeDtypeStruct(control.shape, F32)...  0.76 us

profile of v3, /device:TPU:0, one launch (start us, length us, event | category | flops | bytes accessed | tf_op | source)
XLA Modules:
  0.0 17.6 jit_solution(11297584790594350709)
XLA Ops:
  0.6 16.2 %shard_map.104 = (f32[3,4,32,128]{3,2,1,0:T(8,128)S(1)}, f32[3,4,32,128]{3,2,1,0:T(8,128)S(1)}) custom-call(f32[3,4,32,128]{3,2,1,0:T(8,128)} %control_hbm.1, f32[3,4,32,128]{3,2,1,0:T(8,128)} %gradient_hbm.1, f32[3,32,128]{2,1,0:T(8,128)} %std_hbm.1, s32[32,128]{1,0:T(8,128)} %mask_hbm.1, f32[3,21]{1,0:T(4,128)} %xt_hbm.1, f32[3,21]{1,0:T(4,128)} %yt_hbm.1, ...), custom_call_target="tpu_custom_call" | custom-call | tf_op jit(solution)/shard_map/pallas_call | solution.py:484
  16.8 0.8 %shard_map.105 = (f32[3,4,32,128]{3,2,1,0:T(8,128)}, f32[3,4,32,128]{3,2,1,0:T(8,128)}) custom-call(f32[3,4,32,128]{3,2,1,0:T(8,128)S(1)} %get-tuple-element.4.inc, f32[3,4,32,128]{3,2,1,0:T(8,128)S(1)} %get-tuple-element.5.cg), custom_call_target="tpu_custom_call" | custom-call | tf_op jit(solution)/shard_map/pallas_call | solution.py:524
